TPU v7x, 256 devices: a whole 4x4x8 slice. The times are simulated.
256 devices in a mesh: ind: 64 (over z_hi, y, x, core), snp: 4 (over z_lo).
Axes of the slice: x: 4, y: 4, z: 8 (z_hi: 2, z_lo: 4; z = z_hi * 4 + z_lo), core: 2. Of those that a mesh axis runs over, the one named last changes fastest.
Arguments:
- dosages: bfloat16 [11264, 131072], P('ind', 'snp'), may hold values from 0 to 2, as said below
- phenotype: int32 [11264], P('ind'), may hold values 0 or 1
- mean_effect: float32 [131072], P(('snp', 'ind')), may hold values from -3 to 3
- factor: float32 [131072, 256], P(('snp', 'ind')), may hold values from -1 to 1
- log_scale: float32 [131072], P(('snp', 'ind')), may hold values from -1 to 0
- diag_noise: float32 [131072, 128], P(('snp', 'ind')), may hold values from -5 to 5
- base_points: float32 [128, 256], replicated, may hold values from -5 to 5
Outputs:
- grad_mean: float32 [131072], P(('snp', 'ind'))
- grad_factor: float32 [131072, 256], P(('snp', 'ind'))
- grad_log_scale: float32 [131072], P(('snp', 'ind'))
- mean_loglik: float32 [], replicated
- rank_entropy: float32 [], replicated
Inputs may be any that keep to these rules, and one draw needn't show every extreme that they name: `dosages`: each entry is an allele count.
All inputs are finite; a program needn't handle non-finite values. No bound on the sum of `phenotype` on one device may be relied on, other than what follows from the above.
Results may differ from a plain program's by a relative error of at most 0.00085.
The roundings to bfloat16 on the way count: a program that leaves them out, or rounds other values in their place, can miss the bound.
Values may be sent and summed in bfloat16 or wider, within the bound.
No kernel may reach another device: no remote copies, remote signals or barrier semaphores. Data moves between devices by JAX's collectives and lax.ppermute only.
A program may use at most 128 MiB of HBM per device.

v0:
```python
import math

import jax
import jax.numpy as jnp
from jax import lax
from jax.sharding import PartitionSpec as P

P_SIZE = 131072
R = 256
S = 128
COHORT_RATIO = 40


def invert_gram(gram_matrix):
    factor_chol = jnp.linalg.cholesky(gram_matrix)
    identity = jnp.eye(gram_matrix.shape[0], dtype=gram_matrix.dtype)
    lower_inv = lax.linalg.triangular_solve(factor_chol, identity, left_side=True, lower=True)
    inverse = jnp.dot(lower_inv.T, lower_inv, precision=lax.Precision.HIGHEST)
    return (factor_chol, inverse)


def on_device(dosages, phenotype, mean_effect, factor, log_scale, diag_noise, base_points):
    sample_count = base_points.shape[0]
    local_ind = dosages.shape[0]
    total_ind = local_ind * lax.axis_size("ind")
    root_p = math.sqrt(P_SIZE)
    spread = jnp.exp(log_scale)
    low_rank = jnp.dot(factor, base_points.T, precision=lax.Precision.HIGHEST)
    samples = ((mean_effect[:, None] + low_rank + spread[:, None] * diag_noise) / root_p).astype(
        jnp.bfloat16
    )
    columns = dosages
    partial_logits = jnp.dot(
        columns,
        lax.all_gather(samples, "ind", axis=0, tiled=True),
        preferred_element_type=jnp.float32,
    )
    labels = phenotype.astype(jnp.float32)[:, None]
    logits = lax.psum(partial_logits.astype(jnp.bfloat16), "snp").astype(jnp.float32)
    loglik_terms = jnp.sum(labels * logits - jax.nn.softplus(logits))
    loglik_total = lax.psum(loglik_terms, "ind")
    weights = (COHORT_RATIO * (labels - jax.nn.sigmoid(logits)) / S).astype(jnp.bfloat16)
    mean_loglik = loglik_total / (total_ind * sample_count)
    columns = dosages
    gradient = lax.psum_scatter(
        lax.dot_general(
            columns, weights, (((0,), (0,)), ((), ())), preferred_element_type=jnp.float32
        ),
        "ind",
        scatter_dimension=0,
        tiled=True,
    )
    scaled = factor / spread[:, None]
    identity = jnp.eye(R, dtype=jnp.float32)
    gram_part = jnp.dot(scaled.T, scaled, precision=lax.Precision.HIGHEST)
    gram_matrix = identity + lax.psum(gram_part, ("ind", "snp"))
    factor_chol, inverse = invert_gram(gram_matrix)
    rank_entropy = jnp.sum(jnp.log(jnp.diagonal(factor_chol))) / R
    projected = jnp.dot(factor, inverse, precision=lax.Precision.HIGHEST)
    spread_sq = spread * spread
    grad_mean = jnp.sum(gradient, axis=1) / root_p - mean_effect
    grad_factor = (
        jnp.dot(gradient, base_points, precision=lax.Precision.HIGHEST) / root_p
        - factor
        + projected / spread_sq[:, None]
    )
    leverage = jnp.sum(projected * factor, axis=1)
    grad_log_scale = (
        spread * jnp.sum(gradient * diag_noise, axis=1) / root_p
        + 1.0
        - spread_sq
        - leverage / spread_sq
    )
    return (grad_mean, grad_factor, grad_log_scale, mean_loglik, rank_entropy)


def solution(mesh):
    in_specs = (
        P("ind", "snp"),
        P("ind"),
        P(("snp", "ind")),
        P(("snp", "ind"), None),
        P(("snp", "ind")),
        P(("snp", "ind"), None),
        P(),
    )
    out_specs = (P(("snp", "ind")), P(("snp", "ind"), None), P(("snp", "ind")), P(), P())
    return jax.shard_map(
        on_device, mesh=mesh, in_specs=in_specs, out_specs=out_specs, check_vma=False
    )
```

profile of v0, /device:TPU:32, one launch (start us, length us, event | category | flops | bytes accessed | tf_op | source)
XLA Modules:
  0.0 618.1 jit_solution(5039435738711736244)
XLA Ops:
  8.0 0.0 all-gather.2.cloned.1.call-start
  8.1 0.7 exp.10
  8.8 0.1 copy-done
  8.9 2.4 fusion.4
  11.3 0.0 all-gather.2.cloned.1.call-update
  11.3 0.0 all-reduce.3.cloned.1.call-start
  11.3 3.1 fusion.6
  14.4 0.0 all-reduce.3.cloned.1.call-update
  14.4 0.0 reduce-scatter.2.cloned.1.call-start
  14.5 0.7 convert_element_type.24
  15.2 112.5 %all-gather.2.cloned.1.call-done = bf16[32768,128]{1,0:T(8,128)(2,1)} async-done(((bf16[512,128]{1,0:T(8,128)(2,1)}), bf16[32768,128]{1,0:T(8,128)(2,1)}) %all-gather.2.cloned.1.call-update) | async-done | bytes 8388624 | tf_op jit(solution)/shard_map/all_gather | solution.py:35
  127.6 9.9 %fusion.5 = bf16[176,128]{1,0:T(8,128)(2,1)S(1)} fusion(bf16[176,32768]{1,0:T(8,128)(2,1)} %param.7, bf16[32768,128]{1,0:T(8,128)(2,1)} %all-gather.2.cloned.1.call-done), kind=kOutput, calls=%fused_computation.15 | convolution fusion | flops 1476417536 | bytes 19968000 | tf_op jit(solution)/shard_map/dot_general | solution.py:33
  137.5 15.6 %psum.21 = bf16[176,128]{1,0:T(8,128)(2,1)S(1)} all-reduce(bf16[176,128]{1,0:T(8,128)(2,1)S(1)} %fusion.5), channel_id=1, replica_groups=mesh['ind'=64,'snp'=4] {'snp'}, use_global_device_ids=true, to_apply=%region_0.0 | all-reduce | flops 22528 | bytes 90112 | tf_op jit(solution)/shard_map/psum | solution.py:39
  153.1 12.5 %convolution_bitcast_fusion = f32[32768,128]{0,1:T(8,128)} fusion(bf16[176,32768]{1,0:T(8,128)(2,1)} %param.7, bf16[176,128]{1,0:T(8,128)(2,1)S(1)} %psum.21, f32[176]{0:T(256)S(1)} %convert_element_type.24), kind=kOutput, calls=%fused_computation.3 | convolution fusion | flops 1476552704 | bytes 28357312 | tf_op jit(solution)/shard_map/dot_general | solution.py:46
  165.6 0.0 reduce-scatter.2.cloned.1.call-update
  165.6 0.9 copy-done.2
  166.5 0.1 copy.19
  166.7 122.0 %all-reduce.3.cloned.1.call-done = f32[256,256]{0,1:T(8,128)} async-done(((f32[256,256]{0,1:T(8,128)}), f32[256,256]{0,1:T(8,128)}) %all-reduce.3.cloned.1.call-update) | async-done | bytes 262160 | tf_op jit(solution)/shard_map/psum | solution.py:56
  288.7 1.0 convert_add_fusion
  289.7 0.1 copy.17
  289.8 1.0 fusion.12
  290.8 11.7 %cholesky.50 = f32[128,128]{1,0:T(8,128)S(1)} custom-call(f32[128,128]{1,0:T(8,128)S(1)} %cholesky.118), custom_call_target="Cholesky" | custom-call | tf_op jit(solution)/shard_map/jit(cholesky)/cholesky | solution.py:15
  302.6 9.8 %custom-call.14 = f32[1,128,128]{1,2,0:T(8,128)S(1)} custom-call(f32[1,128,128]{2,1,0:T(8,128)S(1)} %get-tuple-element.30), custom_call_target="InvertDiagBlocksLowerTriangular" | custom-call | tf_op jit(solution)/shard_map/jit(cholesky)/cholesky | solution.py:15
  312.4 0.2 constant_dynamic-update-slice_fusion.1
  312.6 0.3 convolution_subtract_fusion.1
  312.9 11.9 %cholesky.105 = f32[128,128]{1,0:T(8,128)S(1)} custom-call(f32[128,128]{1,0:T(8,128)S(1)} %convolution_subtract_fusion.1), custom_call_target="Cholesky" | custom-call | tf_op jit(solution)/shard_map/jit(cholesky)/cholesky | solution.py:15
  324.8 0.6 compare_reduce_fusion.1
  325.5 0.6 compare_reduce_fusion
  327.5 0.1 triangular_solve.64
  327.5 4.0 while.1
  327.5 0.6 fusion.57
  328.1 1.4 bitcast_dynamic-update-slice_fusion.2
  329.5 0.6 fusion.57
  330.1 1.4 bitcast_dynamic-update-slice_fusion.2
  331.5 19.7 %custom-call.15 = f32[2,128,128]{1,2,0:T(8,128)S(1)} custom-call(f32[2,128,128]{2,1,0:T(8,128)S(1)} %get-tuple-element.12), custom_call_target="InvertDiagBlocksLowerTriangular" | custom-call | tf_op jit(solution)/shard_map/triangular_solve | solution.py:17
  351.2 2.3 gather_fusion
  353.6 0.6 log_reduce_fusion
  354.2 0.3 fusion.15
  354.4 0.4 convolution_subtract_fusion
  354.8 0.3 fusion.31
  355.1 0.6 fusion.8
  355.8 0.7 multiply_reduce_fusion
  356.4 0.7 fusion.25
  357.8 208.4 %psum.23 = f32[]{:T(128)} all-reduce(f32[]{:T(128)} %fusion.25), channel_id=1, replica_groups=mesh['ind'=64,'snp'=4] {'ind'}, use_global_device_ids=true, to_apply=%region_11.12 | all-reduce | flops 1 | bytes 8 | tf_op jit(solution)/shard_map/psum | solution.py:41
  566.9 37.5 %reduce-scatter.2.cloned.1.call-done = f32[512,128]{0,1:T(8,128)} async-done(((f32[32768,128]{0,1:T(8,128)}), f32[512,128]{0,1:T(8,128)}) %reduce-scatter.2.cloned.1.call-update) | async-done | bytes 262160 | tf_op jit(solution)/shard_map/reduce_scatter | solution.py:45
  604.4 1.0 multiply_reduce_fusion.1
  605.4 0.6 divide_subtract_fusion
  606.0 2.4 fusion.1
  (20 shorter events, 0.2 us)
Async XLA Ops:
  8.0 0.9 copy-start
  8.0 119.6 %all-gather.2.cloned.1.call-start = ((), (), s32[]{:S(2)}) async-start(), calls=%async_computation.1 | async-start | bytes 8519680 | tf_op jit(solution)/shard_map/all_gather | solution.py:35
  11.3 277.4 %all-reduce.3.cloned.1.call-start = ((), (), s32[]{:S(2)}) async-start(), calls=%async_computation.3 | async-start | bytes 524288 | tf_op jit(solution)/shard_map/psum | solution.py:56
  14.4 589.9 %reduce-scatter.2.cloned.1.call-start = ((), (), s32[]{:S(2)}) async-start(), calls=%async_computation.2 | async-start | bytes 17039360 | tf_op jit(solution)/shard_map/reduce_scatter | solution.py:45
  165.6 0.9 copy-start.2
  165.6 190.2 %copy-start.1 = (f32[512,256]{1,0:T(8,128)S(1)}, f32[512,256]{1,0:T(8,128)}, u32[]{:S(2)}) copy-start(f32[512,256]{1,0:T(8,128)} %param.10) | copy-start | bytes 1572868
  165.6 439.8 %copy-start.3 = (f32[512]{0:T(512)S(1)}, f32[512]{0:T(512)}, u32[]{:S(2)}) copy-start(f32[512]{0:T(512)} %param.9) | copy-start | bytes 6148
  165.6 439.8 %copy-start.4 = (f32[512]{0:T(512)S(1)}, f32[512]{0:T(512)}, u32[]{:S(2)}) copy-start(f32[512]{0:T(512)} %param.11) | copy-start | bytes 6148
Sparse Core Ops, SparseCore 0:
  12.5 115.0 all-gather.1
  165.7 438.5 reduce-scatter.1
Sparse Core Ops, SparseCore 1:
  17.8 270.9 all-reduce.2
where the time goes:
time: 619 us; the launch traced here: 618 us
  waiting for transfers between devices  272 us (44%)
  blocking collectives  224 us (36%)
  other arithmetic  60.1 us (10%)
  matrix products  32.9 us (5%)
  between operations  20.6 us (3%)
  local copies, waits for them, and re-layouts  8.42 us (1%)
    psum x1, blocking collectives, on_device(): loglik_total = lax.psum(loglik_terms, 'ind')  208 us
    psum x1, waiting for transfers between devices, on_device(): gram_matrix = identity + lax.psum(gram_part, ('ind', 'snp'))  122 us
    all_gather x1, waiting for transfers between devices, on_device(): lax.all_gather(samples, 'ind', axis=0, tiled=True)  112 us
    reduce_scatter x1, waiting for transfers between devices, on_device(): lax.psum_scatter(lax.dot_general(columns, weights, (((0,), (0,)), ((), ()...  37.5 us
    another operation x7, other arithmetic, invert_gram(): factor_chol = jnp.linalg.cholesky(gram_matrix)  34.8 us
    another operation x3, other arithmetic, invert_gram(): lax.linalg.triangular_solve(factor_chol, identity, left_side=True, lower=...  19.7 us
    psum x1, blocking collectives, on_device(): lax.psum(partial_logits.astype(jnp.bfloat16), 'snp').astype(jnp.float32)  15.6 us
    dot_general x1, matrix products, on_device(): lax.dot_general(columns, weights, (((0,), (0,)), ((), ())), preferred_ele...  12.5 us
  transfers between devices with their start and end apart: 3, of which 3 were waited for; matrix products, arithmetic and copies ran while one was open for 15% of the time, Pallas kernels for 0%

commit v1 on v0

v1 whole, which is shorter than its diff:
```python
import math

import jax
import jax.numpy as jnp
from jax import lax
from jax.experimental import pallas as pl
from jax.experimental.pallas import tpu as pltpu
from jax.sharding import Mesh
from jax.sharding import PartitionSpec as P

P_SIZE = 131072
R = 256
S = 128
COHORT_RATIO = 40
IND = ("zh", "y", "x", "c")
HIGHEST = lax.Precision.HIGHEST
F32, BF16, F16 = jnp.float32, jnp.bfloat16, jnp.float16
BLOCK = 256
BUNDLE = 8 * BLOCK
VMEM_LIMIT = 48 * 1024 * 1024


def receive(a, axis, k, n):
    return lax.ppermute(a, axis, [((i + k) % n, i) for i in range(n)])


def sum4(a, axis):
    r2, r1, r3 = (receive(a, axis, k, 4) for k in (2, 1, 3))
    return (a + r2) + (r1 + r3)


def extract_body(where, d_ref, out_ref, sem):
    zh, y, x, c = where[0], where[1], where[2], where[3]
    for j in range(8):
        k, half = j // 2, j % 2
        for i in range(8):
            dz, dn = i // 4, i % 4
            dy, dx = (k, dn) if half == 0 else (dn, k)
            chip = (((zh + dz) % 2) * 4 + (y + dy) % 4) * 4 + (x + dx) % 4
            start = pl.multiple_of(chip * 1024 + c * 512 + half * BLOCK, BLOCK)
            pltpu.make_async_copy(
                d_ref.at[:, pl.ds(start, BLOCK)],
                out_ref.at[:, pl.ds((j * 8 + i) * BLOCK, BLOCK)],
                sem,
            ).start()
    pltpu.make_async_copy(out_ref, out_ref, sem).wait()


def extract(dosages, where):
    rows, columns = dosages.shape
    return pl.pallas_call(
        extract_body,
        out_shape=jax.ShapeDtypeStruct((rows, columns // 2), dosages.dtype),
        in_specs=[
            pl.BlockSpec(memory_space=pltpu.SMEM),
            pl.BlockSpec(memory_space=pl.ANY),
        ],
        out_specs=pl.BlockSpec(memory_space=pl.ANY),
        scratch_shapes=[pltpu.SemaphoreType.DMA],
        cost_estimate=pl.CostEstimate(
            flops=0, bytes_accessed=rows * columns * 2, transcendentals=0
        ),
        name="extract",
    )(where, dosages)


def logits_body(n, own_ref, oth_ref, *refs):
    bundles, (in_own, in_oth), (acc_own, acc_oth) = refs[:n], refs[n : n + 2], refs[n + 2 :]
    step = pl.program_id(0)

    @pl.when(step == 0)
    def _():
        acc_own[...] = in_own[...]
        acc_oth[...] = in_oth[...]

    for g in range(n):

        @pl.when(step == g)
        def _():
            block = bundles[g][...]
            acc_own[...] += jnp.dot(own_ref[...], block, preferred_element_type=F32)
            acc_oth[...] += jnp.dot(oth_ref[...], block, preferred_element_type=F32)


def logits_part(own, oth, bundles, first, acc):
    rows = own.shape[0]
    n = len(bundles)
    whole = lambda shape: pl.BlockSpec(shape, lambda g: (0,) * len(shape))
    d_spec = pl.BlockSpec((rows, BUNDLE), lambda g: (0, first + g))
    out = jax.ShapeDtypeStruct((rows, S), F32)
    return pl.pallas_call(
        lambda *refs: logits_body(n, *refs),
        grid=(n,),
        out_shape=(out, out),
        in_specs=[d_spec, d_spec] + [whole((BUNDLE, S))] * n + [whole((rows, S))] * 2,
        out_specs=(whole((rows, S)), whole((rows, S))),
        compiler_params=pltpu.CompilerParams(vmem_limit_bytes=VMEM_LIMIT),
        cost_estimate=pl.CostEstimate(
            flops=4 * rows * S * BUNDLE * n,
            bytes_accessed=n * (rows * BUNDLE * 4 + BUNDLE * S * 2),
            transcendentals=0,
        ),
        name="logits_part",
    )(own, oth, *[b.reshape(BUNDLE, S) for b in bundles], *acc)


def gradient_body(own_ref, oth_ref, w_own, w_oth, out_a, out_b):
    step = pl.program_id(0)
    for g, out in enumerate((out_a, out_b)):

        @pl.when(step == g)
        def _():
            for b in range(8):
                cols = slice(b * BLOCK, (b + 1) * BLOCK)
                part = jnp.dot(w_own[...], own_ref[:, cols], preferred_element_type=F32)
                part += jnp.dot(w_oth[...], oth_ref[:, cols], preferred_element_type=F32)
                out[b] = part


def gradient_part(own, oth, w_own, w_oth, k):
    rows = own.shape[0]
    d_spec = pl.BlockSpec((rows, BUNDLE), lambda g: (0, 2 * k + g))
    w_spec = pl.BlockSpec((S, rows), lambda g: (0, 0))
    out = jax.ShapeDtypeStruct((8, S, BLOCK), F32)
    out_spec = pl.BlockSpec((8, S, BLOCK), lambda g: (0, 0, 0))
    return pl.pallas_call(
        gradient_body,
        grid=(2,),
        out_shape=(out, out),
        in_specs=[d_spec, d_spec, w_spec, w_spec],
        out_specs=(out_spec, out_spec),
        compiler_params=pltpu.CompilerParams(vmem_limit_bytes=VMEM_LIMIT),
        cost_estimate=pl.CostEstimate(
            flops=8 * rows * S * BUNDLE,
            bytes_accessed=rows * BUNDLE * 8 + 16 * S * BLOCK * 4,
            transcendentals=0,
        ),
        name="gradient_part",
    )(own, oth, w_own, w_oth)


def gather_samples(own_rows):
    both = jnp.stack([own_rows, receive(own_rows, "zh", 1, 2)])
    a, b = both[:, :BLOCK], both[:, BLOCK:]
    ax = jnp.stack([a] + [receive(a, "x", k, 4) for k in (1, 2, 3)], axis=1)
    by = jnp.stack([b] + [receive(b, "y", k, 4) for k in (1, 2, 3)], axis=1)
    bundles = [(ax, by)]
    for k in (1, 2, 3):
        bundles.append((receive(ax, "y", k, 4), receive(by, "x", k, 4)))
    return bundles


def reduce_half(pieces, first_axis, second_axis):
    sent = lambda k: pieces[k].astype(F16)
    r1, r2, r3 = (receive(sent(k), first_axis, -k, 4).astype(F32) for k in (1, 2, 3))
    part = ((pieces[0] + r2) + (r1 + r3)).reshape(2, 4, S, BLOCK)
    sent = part[:, 1:].astype(F16)
    r1, r2, r3 = (receive(sent[:, k - 1], second_axis, -k, 4).astype(F32) for k in (1, 2, 3))
    return (part[:, 0] + r2) + (r1 + r3)


def sum_gram(part, c, x):
    half = R // 2
    mine = lax.dynamic_slice_in_dim(part, c * half, half, 0)
    other = lax.dynamic_slice_in_dim(part, (1 - c) * half, half, 0)
    rows = mine + receive(other, "c", 1, 2)
    quarter = half // 4
    piece = lambda k: lax.dynamic_slice_in_dim(rows, ((x - k) % 4) * quarter, quarter, 0)
    r1, r2, r3 = (receive(piece(k), "x", k, 4) for k in (1, 2, 3))
    total = (piece(0) + r2) + (r1 + r3)
    total = sum4(sum4(total, "y"), "snp")
    total = total + receive(total, "zh", 1, 2)
    parts = jnp.stack([total] + [receive(total, "x", k, 4) for k in (1, 2, 3)])
    rows = jnp.roll(parts, x, axis=0).reshape(half, R)
    other = receive(rows, "c", 1, 2)
    return jnp.where(c == 0, jnp.concatenate([rows, other]), jnp.concatenate([other, rows]))


def invert_gram(gram):
    h = R // 2
    eye = jnp.eye(h, dtype=F32)
    dot = lambda a, b: jnp.dot(a, b, precision=HIGHEST)
    solve = lambda l: lax.linalg.triangular_solve(l, eye, left_side=True, lower=True)
    l11 = lax.linalg.cholesky(gram[:h, :h], symmetrize_input=False)
    i11 = solve(l11)
    l21 = dot(gram[h:, :h], i11.T)
    l22 = lax.linalg.cholesky(gram[h:, h:] - dot(l21, l21.T), symmetrize_input=False)
    i22 = solve(l22)
    i21 = -dot(i22, dot(l21, i11))
    top = jnp.concatenate([dot(i11.T, i11) + dot(i21.T, i21), dot(i21.T, i22)], axis=1)
    bottom = jnp.concatenate([dot(i22.T, i21), dot(i22.T, i22)], axis=1)
    inverse = jnp.concatenate([top, bottom], axis=0)
    return jnp.concatenate([jnp.diagonal(l11), jnp.diagonal(l22)]), inverse


def on_device(dosages, phenotype, mean_effect, factor, log_scale, diag_noise, base_points):
    zh, y, x, c = (lax.axis_index(a) for a in IND)
    total_ind = dosages.shape[0] * 64
    root_p = math.sqrt(P_SIZE)
    scale = 2.0 ** math.floor(math.log2(65504 * S / (2 * COHORT_RATIO * total_ind)))

    spread = jnp.exp(log_scale)
    low_rank = jnp.dot(factor, base_points.T, precision=HIGHEST)
    samples = ((mean_effect[:, None] + low_rank + spread[:, None] * diag_noise) / root_p).astype(
        BF16
    )
    where = jnp.stack([zh, y, x, 1 - c]).astype(jnp.int32)
    for_other = extract(dosages, where)
    oth = receive(for_other, "c", 1, 2)
    own = extract(dosages, jnp.stack([zh, y, x, c]).astype(jnp.int32))

    bundles = gather_samples(samples)
    zero = jnp.zeros((dosages.shape[0], S), F32)
    acc = logits_part(own, oth, list(bundles[0]), 0, (zero, zero))
    acc = logits_part(own, oth, [b for k in (1, 2, 3) for b in bundles[k]], 2, acc)

    scaled = factor / spread[:, None]
    gram_part = jnp.dot(scaled.T, scaled, precision=HIGHEST)
    gram = jnp.eye(R, dtype=F32) + sum_gram(gram_part, c, x)

    block_logits = (acc[0] + receive(acc[1], "c", 1, 2)).astype(BF16)
    r1, r2, r3 = (receive(block_logits, "snp", k, 4).astype(F32) for k in (1, 2, 3))
    logits = (block_logits.astype(F32) + r2) + (r1 + r3)
    labels = phenotype.astype(F32)[:, None]
    weights = (COHORT_RATIO * (labels - jax.nn.sigmoid(logits)) / S).astype(BF16)
    w_own = (weights * scale).astype(BF16).T
    w_oth = receive(w_own, "c", 1, 2)
    pieces = [gradient_part(own, oth, w_own, w_oth, k) for k in (0, 1, 2, 3)]
    half_a = reduce_half([p[0] for p in pieces], "y", "x")
    half_b = reduce_half([p[1] for p in pieces], "x", "y")
    both = jnp.concatenate([half_a, half_b], axis=-1)
    gradient = (both[0] + receive(both[1], "zh", 1, 2)) * (1.0 / scale)

    loglik = jnp.full((8, 128), jnp.sum(labels * logits - jax.nn.softplus(logits)))
    loglik = sum4(sum4(loglik, "x"), "y")
    loglik = loglik + receive(loglik, "zh", 1, 2)
    loglik = loglik + receive(loglik, "c", 1, 2)
    mean_loglik = loglik[0, 0] / (total_ind * S)

    diagonal, inverse = invert_gram(gram)
    rank_entropy = jnp.sum(jnp.log(diagonal)) / R
    projected = jnp.dot(factor, inverse, precision=HIGHEST)
    spread_sq = spread * spread
    grad_mean = jnp.sum(gradient, axis=0) / root_p - mean_effect
    grad_factor = (
        lax.dot_general(gradient, base_points, (((0,), (0,)), ((), ())), precision=HIGHEST) / root_p
        - factor
        + projected / spread_sq[:, None]
    )
    leverage = jnp.sum(projected * factor, axis=1)
    grad_log_scale = (
        spread * jnp.sum(gradient * diag_noise.T, axis=0) / root_p
        + 1.0
        - spread_sq
        - leverage / spread_sq
    )
    return (grad_mean, grad_factor, grad_log_scale, mean_loglik, rank_entropy)


def solution(mesh):
    fine = Mesh(mesh.devices.reshape(2, 4, 4, 2, 4), IND + ("snp",))
    rows = ("snp",) + IND
    in_specs = (P(IND, "snp"), P(IND), P(rows), P(rows, None), P(rows), P(rows, None), P())
    out_specs = (P(rows), P(rows, None), P(rows), P(), P())
    return jax.shard_map(
        on_device, mesh=fine, in_specs=in_specs, out_specs=out_specs, check_vma=False
    )
```

time: 619 us -> 601 us (0.971); the launches traced: 618 us -> 592 us
  Pallas kernels: 0 us -> 371 us
  blocking collectives: 224 us -> 0 us
  waiting for transfers between devices: 272 us -> 58.4 us
  starting transfers between devices: 0.12 us -> 82.1 us
  matrix products: 32.9 us -> 11.1 us
  between operations: 20.6 us -> 5.38 us
  other arithmetic: 60.1 us -> 53.8 us
    pallas_call x0 -> x8, Pallas kernels: none -> 371 us  [the longest x2 353 us: extract(): pl.pallas_call(extract_body, out_shape=jax.ShapeDtypeStruct((rows, column...]
    psum x2 -> x0, blocking collectives: 224 us -> none  [the longest x1 208 us: on_device(): loglik_total = lax.psum(loglik_terms, 'ind')]
    psum x1 -> x0, waiting for transfers between devices: 122 us -> none  [on_device(): gram_matrix = identity + lax.psum(gram_part, ('ind', 'snp'))]
    all_gather x1 -> x0, waiting for transfers between devices: 112 us -> none  [on_device(): lax.all_gather(samples, 'ind', axis=0, tiled=True)]
    ppermute x0 -> x55, starting transfers between devices: none -> 82.1 us  [receive(): return lax.ppermute(a, axis, [((i + k) % n, i) for i in range(n)])]
    ppermute x0 -> x55, waiting for transfers between devices: none -> 58.4 us  [receive(): return lax.ppermute(a, axis, [((i + k) % n, i) for i in range(n)])]
    reduce_scatter x1 -> x0, waiting for transfers between devices: 37.5 us -> none  [on_device(): lax.psum_scatter(lax.dot_general(columns, weights, (((0,), (0,)), ((), ()...]
    dot_general x7 -> x13, matrix products: 31.4 us -> 10.6 us  [the longest x9 4.27 us: invert_gram(): dot = lambda a, b: jnp.dot(a, b, precision=HIGHEST)]
  transfers between devices with their start and end apart: 3 -> 55, of which waited for: 3 -> 22; matrix products, arithmetic and copies ran while one was open for 15% -> 12% of each run, Pallas kernels for 0% -> 61%
where the time goes in v1:
time: 601 us; the launch traced here: 592 us
  Pallas kernels  371 us (62%)
  starting transfers between devices  82.1 us (14%)
  waiting for transfers between devices  58.4 us (10%)
  other arithmetic  53.8 us (9%)
  matrix products  11.1 us (2%)
  local copies, waits for them, and re-layouts  9.6 us (2%)
    pallas_call x2, Pallas kernels, extract(): pl.pallas_call(extract_body, out_shape=jax.ShapeDtypeStruct((rows, column...  353 us
    ppermute x55, starting transfers between devices, receive(): return lax.ppermute(a, axis, [((i + k) % n, i) for i in range(n)])  82.1 us
    ppermute x55, waiting for transfers between devices, receive(): return lax.ppermute(a, axis, [((i + k) % n, i) for i in range(n)])  58.4 us
    another operation x4, other arithmetic, invert_gram(): lax.linalg.triangular_solve(l, eye, left_side=True, lower=True)  20.9 us
    another operation x3, other arithmetic, invert_gram(): l11 = lax.linalg.cholesky(gram[:h, :h], symmetrize_input=False)  12.4 us
    another operation x3, other arithmetic, invert_gram(): lax.linalg.cholesky(gram[h:, h:] - dot(l21, l21.T), symmetrize_input=False)  12.4 us
  transfers between devices with their start and end apart: 55, of which 22 were waited for; matrix products, arithmetic and copies ran while one was open for 12% of the time, Pallas kernels for 61%

profile of v1, /device:TPU:32, one launch (start us, length us, event | category | flops | bytes accessed | tf_op | source)
XLA Modules:
  0.0 591.7 jit_solution(6160229310638517930)
XLA Ops:
  1.4 2.4 fusion.5
  4.5 176.6 %extract.3 = bf16[176,16384]{1,0:T(8,128)(2,1)} custom-call(s32[4]{0:T(128)} %get-tuple-element.40.where, bf16[176,32768]{1,0:T(8,128)(2,1)} %d_ref.3), custom_call_target="tpu_custom_call" | custom-call | bytes 11534336 | tf_op jit(solution)/shard_map/extract/pallas_call | solution.py:51
  181.8 2.8 collective-permute-start.34
  184.6 2.3 collective-permute-start.33
  186.9 2.8 collective-permute-done.35
  190.1 3.1 collective-permute-start.37
  193.2 2.2 collective-permute-start.36
  196.0 6.4 %collective-permute-start.1 = (bf16[512,128]{1,0:T(8,128)(2,1)S(1)}, bf16[512,128]{1,0:T(8,128)(2,1)S(1)}, u32[]{:S(2)}, u32[]{:S(2)}) collective-permute-start(bf16[512,128]{1,0:T(8,128)(2,1)S(1)} %fusion.4), channel_id=1, source_target_pairs={{128,0},{0,128},{129,1},{1,129},{130,2},{2,130},{131,3},{3,131},{1... | collective-permute-start | bytes 393224 | tf_op jit(solution)/shard_map/ppermute | solution.py:24
  204.5 3.3 collective-permute-start.39
  210.1 3.1 collective-permute-start.42
  213.3 176.6 %extract.2.refs_0_.own_ref = bf16[176,16384]{1,0:T(8,128)(2,1)} custom-call(s32[4]{0:T(128)} %pad_add_fusion.where, bf16[176,32768]{1,0:T(8,128)(2,1)} %d_ref.3), custom_call_target="tpu_custom_call" | custom-call | bytes 11534336 | tf_op jit(solution)/shard_map/extract/pallas_call | solution.py:51
  390.0 2.9 collective-permute-start.43
  394.7 1.8 collective-permute-start.2
  396.4 2.9 collective-permute-start.44
  399.3 2.8 collective-permute-done.44
  402.7 4.6 collective-permute-done.45
  408.8 2.7 collective-permute-start.7
  415.8 2.3 collective-permute-start.10
  418.1 1.7 collective-permute-start.9
  420.5 11.7 %custom-call.12 = f32[128,128]{1,0:T(8,128)S(1)} custom-call(f32[128,128]{1,0:T(8,128)S(1)} %slice.94), custom_call_target="Cholesky" | custom-call | tf_op jit(solution)/shard_map/cholesky/custom-call.1 | solution.py:184
  433.6 9.8 %custom-call.13 = f32[1,128,128]{1,2,0:T(8,128)S(1)} custom-call(f32[1,128,128]{2,1,0:T(8,128)S(1)} %get-tuple-element.35), custom_call_target="InvertDiagBlocksLowerTriangular" | custom-call | tf_op jit(solution)/shard_map/triangular_solve/custom-call.0 | solution.py:183
  444.2 11.7 %custom-call.14 = f32[128,128]{1,0:T(8,128)S(1)} custom-call(f32[128,128]{1,0:T(8,128)S(1)} %slice_subtract_fusion), custom_call_target="Cholesky" | custom-call | tf_op jit(solution)/shard_map/cholesky/custom-call.1 | solution.py:187
  462.2 6.5 %collective-permute-done.12 = bf16[2,4,256,128]{3,2,0,1:T(8,128)(2,1)S(1)} collective-permute-done((bf16[2,4,256,128]{3,2,0,1:T(8,128)(2,1)S(1)}, bf16[2,4,256,128]{3,2,0,1:T(8,128)(2,1)S(1)}, u32[]{:S(2)}, u32[]{:S(2)}) %collective-permute-start.12) | collective-permute-done | bytes 524320 | tf_op jit(solution)/shard_map/ppermute | solution.py:24
  469.0 2.5 logits_part.2
  471.5 6.5 %logits_part.3 = (f32[176,128]{1,0:T(8,128)S(1)}, f32[176,128]{1,0:T(8,128)S(1)}) custom-call(bf16[176,16384]{1,0:T(8,128)(2,1)} %extract.2.refs_0_.own_ref, bf16[176,16384]{1,0:T(8,128)(2,1)} %collective-permute-done.refs_1_.oth_ref, bf16[2048,128]{1,0:T(8,128)(2,1)S(1)} %bitcast.116, bf16[2048,128]{1,0:T(8,128)(2,1)S(1)} %bitcast.117, ...), custom_call_target="tpu_custom_call" | custom-call | flops 1107296256 | bytes 11796480 | tf_op jit(solution)/shard_map/logits_part/pallas_call | solution.py:91
  478.9 9.8 %custom-call.15 = f32[1,128,128]{1,2,0:T(8,128)S(1)} custom-call(f32[1,128,128]{2,1,0:T(8,128)S(1)} %get-tuple-element.33), custom_call_target="InvertDiagBlocksLowerTriangular" | custom-call | tf_op jit(solution)/shard_map/triangular_solve/custom-call.0 | solution.py:183
  491.0 2.6 collective-permute-start.15
  493.8 2.1 collective-permute-done.16
  495.9 2.3 collective-permute-done.15
  499.7 2.2 gradient_part.7
  502.0 2.2 collective-permute-start.27
  505.6 1.7 collective-permute-start.48
  509.1 7.1 %collective-permute-done.48 = f32[8,128]{1,0:T(8,128)S(1)} collective-permute-done((f32[8,128]{1,0:T(8,128)S(1)}, f32[8,128]{1,0:T(8,128)S(1)}, u32[]{:S(2)}, u32[]{:S(2)}) %collective-permute-start.48) | collective-permute-done | bytes 4128 | tf_op jit(solution)/shard_map/ppermute | solution.py:24
  516.9 2.9 collective-permute-start.51
  521.3 2.2 gradient_part.6
  525.2 2.2 gradient_part.5
  527.8 2.8 collective-permute-start.25
  530.7 1.7 collective-permute-start.21
  533.3 2.1 collective-permute-start.19
  537.2 2.2 gradient_part.4
  539.5 2.0 collective-permute-start.53
  541.5 8.0 %collective-permute-done.25 = f16[8,128,256]{2,1,0:T(8,128)(2,1)S(1)} collective-permute-done((f16[8,128,256]{2,1,0:T(8,128)(2,1)S(1)}, f16[8,128,256]{2,1,0:T(8,128)(2,1)S(1)}, u32[]{:S(2)}, u32[]{:S(2)}) %collective-permute-start.25) | collective-permute-done | bytes 524320 | tf_op jit(solution)/shard_map/ppermute | solution.py:24
  549.5 6.8 %collective-permute-done.20 = f16[8,128,256]{2,1,0:T(8,128)(2,1)S(1)} collective-permute-done((f16[8,128,256]{2,1,0:T(8,128)(2,1)S(1)}, f16[8,128,256]{2,1,0:T(8,128)(2,1)S(1)}, u32[]{:S(2)}, u32[]{:S(2)}) %collective-permute-start.20) | collective-permute-done | bytes 524320 | tf_op jit(solution)/shard_map/ppermute | solution.py:24
  558.6 1.7 collective-permute-start.29
  569.8 2.0 collective-permute-done.22
  571.9 1.8 collective-permute-start.31
  574.7 2.0 multiply_reduce_fusion
  581.6 4.6 collective-permute-done.31
  (178 shorter events, 59.1 us)
Async XLA Ops:
  3.8 178.0 %collective-permute-start.32 = (f32[128,256]{1,0:T(8,128)S(1)}, f32[128,256]{1,0:T(8,128)S(1)}, u32[]{:S(2)}, u32[]{:S(2)}) collective-permute-start(f32[128,256]{1,0:T(8,128)S(1)} %constant_dynamic-slice_fusion.4), channel_id=1, source_target_pairs={{4,0},{0,4},{5,1},{1,5},{6,2},{2,6},{7,3},{3,7},{12,8},{8,12},{13,... | collective-permute-start | bytes 393224 | tf_op jit(solution)/shard_map/ppermute | solution.py:24
  181.2 287.8 %collective-permute-start = (bf16[176,16384]{1,0:T(8,128)(2,1)}, bf16[176,16384]{1,0:T(8,128)(2,1)}, u32[]{:S(2)}, u32[]{:S(2)}) collective-permute-start(bf16[176,16384]{1,0:T(8,128)(2,1)} %extract.3), channel_id=1, source_target_pairs={{4,0},{0,4},{5,1},{1,5},{6,2},{2,6},{7,3},{3,7},{12,8},{8,12},{13,... | collective-permute-start | bytes 17301512 | tf_op jit(solution)/shard_map/ppermute | solution.py:24
  190.1 12.3 %collective-permute-start.37 = (f32[32,256]{1,0:T(8,128)S(1)}, f32[32,256]{1,0:T(8,128)S(1)}, u32[]{:S(2)}, u32[]{:S(2)}) collective-permute-start(f32[32,256]{1,0:T(8,128)S(1)} %add_add_fusion.5), channel_id=1, source_target_pairs={{32,0},{64,32},{96,64},{0,96},{33,1},{65,33},{97,65},{1,97},{34,2}... | collective-permute-start | bytes 98312 | tf_op jit(solution)/shard_map/ppermute | solution.py:24
  193.2 9.2 %collective-permute-start.38 = (f32[32,256]{1,0:T(8,128)S(1)}, f32[32,256]{1,0:T(8,128)S(1)}, u32[]{:S(2)}, u32[]{:S(2)}) collective-permute-start(f32[32,256]{1,0:T(8,128)S(1)} %add_add_fusion.5), channel_id=1, source_target_pairs={{96,0},{0,32},{32,64},{64,96},{97,1},{1,33},{33,65},{65,97},{98,2}... | collective-permute-start | bytes 98312 | tf_op jit(solution)/shard_map/ppermute | solution.py:24
  193.2 9.2 %collective-permute-start.36 = (f32[32,256]{1,0:T(8,128)S(1)}, f32[32,256]{1,0:T(8,128)S(1)}, u32[]{:S(2)}, u32[]{:S(2)}) collective-permute-start(f32[32,256]{1,0:T(8,128)S(1)} %add_add_fusion.5), channel_id=1, source_target_pairs={{64,0},{96,32},{0,64},{32,96},{65,1},{97,33},{1,65},{33,97},{66,2}... | collective-permute-start | bytes 98312 | tf_op jit(solution)/shard_map/ppermute | solution.py:24
  196.0 196.8 %collective-permute-start.1 = (bf16[512,128]{1,0:T(8,128)(2,1)S(1)}, bf16[512,128]{1,0:T(8,128)(2,1)S(1)}, u32[]{:S(2)}, u32[]{:S(2)}) collective-permute-start(bf16[512,128]{1,0:T(8,128)(2,1)S(1)} %fusion.4), channel_id=1, source_target_pairs={{128,0},{0,128},{129,1},{1,129},{130,2},{2,130},{131,3},{3,131},{1... | collective-permute-start | bytes 393224 | tf_op jit(solution)/shard_map/ppermute | solution.py:24
  202.4 6.6 %collective-permute-start.40 = (f32[32,256]{1,0:T(8,128)S(1)}, f32[32,256]{1,0:T(8,128)S(1)}, u32[]{:S(2)}, u32[]{:S(2)}) collective-permute-start(f32[32,256]{1,0:T(8,128)S(1)} %add_add_fusion.4), channel_id=1, source_target_pairs={{1,0},{2,1},{3,2},{0,3},{5,4},{6,5},{7,6},{4,7},{9,8},{10,9},{11,1... | collective-permute-start | bytes 98312 | tf_op jit(solution)/shard_map/ppermute | solution.py:24
  203.5 5.5 collective-permute-start.41
  204.5 5.6 collective-permute-start.39
  210.1 179.8 %collective-permute-start.42 = (f32[32,256]{1,0:T(8,128)S(1)}, f32[32,256]{1,0:T(8,128)S(1)}, u32[]{:S(2)}, u32[]{:S(2)}) collective-permute-start(f32[32,256]{1,0:T(8,128)S(1)} %add_add_fusion.3), channel_id=1, source_target_pairs={{128,0},{0,128},{129,1},{1,129},{130,2},{2,130},{131,3},{3,131},{1... | collective-permute-start | bytes 98312 | tf_op jit(solution)/shard_map/ppermute | solution.py:24
  390.0 6.4 %collective-permute-start.43 = (f32[32,256]{1,0:T(8,128)S(1)}, f32[32,256]{1,0:T(8,128)S(1)}, u32[]{:S(2)}, u32[]{:S(2)}) collective-permute-start(f32[32,256]{1,0:T(8,128)S(1)} %get-tuple-element.38), channel_id=1, source_target_pairs={{8,0},{16,8},{24,16},{0,24},{9,1},{17,9},{25,17},{1,25},{10,2},{18... | collective-permute-start | bytes 98312 | tf_op jit(solution)/shard_map/ppermute | solution.py:24
  392.9 16.0 %collective-permute-start.4 = (bf16[2,256,128]{2,1,0:T(8,128)(2,1)S(1)}, bf16[2,256,128]{2,1,0:T(8,128)(2,1)S(1)}, u32[]{:S(2)}, u32[]{:S(2)}) collective-permute-start(bf16[2,256,128]{2,1,0:T(8,128)(2,1)S(1)} %get-tuple-element.49), channel_id=1, source_target_pairs={{24,0},{0,8},{8,16},{16,24},{25,1},{1,9},{9,17},{17,25},{26,2},{2,... | collective-permute-start | bytes 393224 | tf_op jit(solution)/shard_map/ppermute | solution.py:24
  393.2 18.4 %collective-permute-start.3 = (bf16[2,256,128]{2,1,0:T(8,128)(2,1)S(1)}, bf16[2,256,128]{2,1,0:T(8,128)(2,1)S(1)}, u32[]{:S(2)}, u32[]{:S(2)}) collective-permute-start(bf16[2,256,128]{2,1,0:T(8,128)(2,1)S(1)} %get-tuple-element.49), channel_id=1, source_target_pairs={{16,0},{24,8},{0,16},{8,24},{17,1},{25,9},{1,17},{9,25},{18,2},{26... | collective-permute-start | bytes 393224 | tf_op jit(solution)/shard_map/ppermute | solution.py:24
  394.7 17.2 %collective-permute-start.2 = (bf16[2,256,128]{2,1,0:T(8,128)(2,1)S(1)}, bf16[2,256,128]{2,1,0:T(8,128)(2,1)S(1)}, u32[]{:S(2)}, u32[]{:S(2)}) collective-permute-start(bf16[2,256,128]{2,1,0:T(8,128)(2,1)S(1)} %get-tuple-element.49), channel_id=1, source_target_pairs={{8,0},{16,8},{24,16},{0,24},{9,1},{17,9},{25,17},{1,25},{10,2},{18... | collective-permute-start | bytes 393224 | tf_op jit(solution)/shard_map/ppermute | solution.py:24
  396.4 5.8 collective-permute-start.44
  407.3 6.2 %collective-permute-start.8 = (bf16[2,256,128]{2,1,0:T(8,128)(2,1)S(1)}, bf16[2,256,128]{2,1,0:T(8,128)(2,1)S(1)}, u32[]{:S(2)}, u32[]{:S(2)}) collective-permute-start(bf16[2,256,128]{2,1,0:T(8,128)(2,1)S(1)} %get-tuple-element.48), channel_id=1, source_target_pairs={{96,0},{0,32},{32,64},{64,96},{97,1},{1,33},{33,65},{65,97},{98,2}... | collective-permute-start | bytes 393224 | tf_op jit(solution)/shard_map/ppermute | solution.py:24
  408.8 6.9 %collective-permute-start.7 = (bf16[2,256,128]{2,1,0:T(8,128)(2,1)S(1)}, bf16[2,256,128]{2,1,0:T(8,128)(2,1)S(1)}, u32[]{:S(2)}, u32[]{:S(2)}) collective-permute-start(bf16[2,256,128]{2,1,0:T(8,128)(2,1)S(1)} %get-tuple-element.48), channel_id=1, source_target_pairs={{64,0},{96,32},{0,64},{32,96},{65,1},{97,33},{1,65},{33,97},{66,2}... | collective-permute-start | bytes 393224 | tf_op jit(solution)/shard_map/ppermute | solution.py:24
  411.6 6.5 %collective-permute-start.6 = (bf16[2,256,128]{2,1,0:T(8,128)(2,1)S(1)}, bf16[2,256,128]{2,1,0:T(8,128)(2,1)S(1)}, u32[]{:S(2)}, u32[]{:S(2)}) collective-permute-start(bf16[2,256,128]{2,1,0:T(8,128)(2,1)S(1)} %get-tuple-element.48), channel_id=1, source_target_pairs={{32,0},{64,32},{96,64},{0,96},{33,1},{65,33},{97,65},{1,97},{34,2}... | collective-permute-start | bytes 393224 | tf_op jit(solution)/shard_map/ppermute | solution.py:24
  411.9 8.0 %collective-permute-start.46 = (f32[128,256]{1,0:T(8,128)S(1)}, f32[128,256]{1,0:T(8,128)S(1)}, u32[]{:S(2)}, u32[]{:S(2)}) collective-permute-start(f32[128,256]{1,0:T(8,128)S(1)} %bitcast.124), channel_id=1, source_target_pairs={{4,0},{0,4},{5,1},{1,5},{6,2},{2,6},{7,3},{3,7},{12,8},{8,12},{13,... | collective-permute-start | bytes 393224 | tf_op jit(solution)/shard_map/ppermute | solution.py:24
  413.5 42.5 %collective-permute-start.5 = (bf16[2,4,256,128]{3,2,0,1:T(8,128)(2,1)S(1)}, bf16[2,4,256,128]{3,2,0,1:T(8,128)(2,1)S(1)}, u32[]{:S(2)}, u32[]{:S(2)}) collective-permute-start(bf16[2,4,256,128]{3,2,0,1:T(8,128)(2,1)S(1)} %pad_maximum_fusion), channel_id=1, source_target_pairs={{32,0},{64,32},{96,64},{0,96},{33,1},{65,33},{97,65},{1,97},{34,2}... | collective-permute-start | bytes 1572872 | tf_op jit(solution)/shard_map/ppermute | solution.py:24
  415.8 44.2 %collective-permute-start.10 = (bf16[2,4,256,128]{3,2,0,1:T(8,128)(2,1)S(1)}, bf16[2,4,256,128]{3,2,0,1:T(8,128)(2,1)}, u32[]{:S(2)}, u32[]{:S(2)}) collective-permute-start(bf16[2,4,256,128]{3,2,0,1:T(8,128)(2,1)S(1)} %pad_maximum_fusion), channel_id=1, source_target_pairs={{64,0},{96,32},{0,64},{32,96},{65,1},{97,33},{1,65},{33,97},{66,2}... | collective-permute-start | bytes 1572872 | tf_op jit(solution)/shard_map/ppermute | solution.py:24
  418.1 38.0 %collective-permute-start.9 = (bf16[2,4,256,128]{3,2,0,1:T(8,128)(2,1)S(1)}, bf16[2,4,256,128]{3,2,0,1:T(8,128)(2,1)}, u32[]{:S(2)}, u32[]{:S(2)}) collective-permute-start(bf16[2,4,256,128]{3,2,0,1:T(8,128)(2,1)S(1)} %pad_maximum_fusion.1), channel_id=1, source_target_pairs={{8,0},{16,8},{24,16},{0,24},{9,1},{17,9},{25,17},{1,25},{10,2},{18... | collective-permute-start | bytes 1572872 | tf_op jit(solution)/shard_map/ppermute | solution.py:24
  419.9 41.2 %collective-permute-start.11 = (bf16[2,4,256,128]{3,2,0,1:T(8,128)(2,1)S(1)}, bf16[2,4,256,128]{3,2,0,1:T(8,128)(2,1)}, u32[]{:S(2)}, u32[]{:S(2)}) collective-permute-start(bf16[2,4,256,128]{3,2,0,1:T(8,128)(2,1)S(1)} %pad_maximum_fusion.1), channel_id=1, source_target_pairs={{16,0},{24,8},{0,16},{8,24},{17,1},{25,9},{1,17},{9,25},{18,2},{26... | collective-permute-start | bytes 1572872 | tf_op jit(solution)/shard_map/ppermute | solution.py:24
  456.0 12.7 %collective-permute-start.12 = (bf16[2,4,256,128]{3,2,0,1:T(8,128)(2,1)S(1)}, bf16[2,4,256,128]{3,2,0,1:T(8,128)(2,1)S(1)}, u32[]{:S(2)}, u32[]{:S(2)}) collective-permute-start(bf16[2,4,256,128]{3,2,0,1:T(8,128)(2,1)S(1)} %pad_maximum_fusion), channel_id=1, source_target_pairs={{96,0},{0,32},{32,64},{64,96},{97,1},{1,33},{33,65},{65,97},{98,2}... | collective-permute-start | bytes 1572872 | tf_op jit(solution)/shard_map/ppermute | solution.py:24
  456.1 12.9 %collective-permute-start.13 = (bf16[2,4,256,128]{3,2,0,1:T(8,128)(2,1)S(1)}, bf16[2,4,256,128]{3,2,0,1:T(8,128)(2,1)S(1)}, u32[]{:S(2)}, u32[]{:S(2)}) collective-permute-start(bf16[2,4,256,128]{3,2,0,1:T(8,128)(2,1)S(1)} %pad_maximum_fusion.1), channel_id=1, source_target_pairs={{24,0},{0,8},{8,16},{16,24},{25,1},{1,9},{9,17},{17,25},{26,2},{2,... | collective-permute-start | bytes 1572872 | tf_op jit(solution)/shard_map/ppermute | solution.py:24
  478.1 10.7 %collective-permute-start.14 = (f32[176,128]{0,1:T(8,128)S(1)}, f32[176,128]{0,1:T(8,128)S(1)}, u32[]{:S(2)}, u32[]{:S(2)}) collective-permute-start(f32[176,128]{0,1:T(8,128)S(1)} %copy.39), channel_id=1, source_target_pairs={{4,0},{0,4},{5,1},{1,5},{6,2},{2,6},{7,3},{3,7},{12,8},{8,12},{13,... | collective-permute-start | bytes 270344 | tf_op jit(solution)/shard_map/ppermute | solution.py:24
  489.3 6.7 %collective-permute-start.16 = (bf16[176,128]{0,1:T(8,128)(2,1)S(1)}, bf16[176,128]{0,1:T(8,128)(2,1)S(1)}, u32[]{:S(2)}, u32[]{:S(2)}) collective-permute-start(bf16[176,128]{0,1:T(8,128)(2,1)S(1)} %add_convert_fusion), channel_id=1, source_target_pairs={{1,0},{2,1},{3,2},{0,3},{5,4},{6,5},{7,6},{4,7},{9,8},{10,9},{11,1... | collective-permute-start | bytes 135176 | tf_op jit(solution)/shard_map/ppermute | solution.py:24
  491.0 7.3 %collective-permute-start.15 = (bf16[176,128]{0,1:T(8,128)(2,1)S(1)}, bf16[176,128]{0,1:T(8,128)(2,1)S(1)}, u32[]{:S(2)}, u32[]{:S(2)}) collective-permute-start(bf16[176,128]{0,1:T(8,128)(2,1)S(1)} %add_convert_fusion), channel_id=1, source_target_pairs={{2,0},{3,1},{0,2},{1,3},{6,4},{7,5},{4,6},{5,7},{10,8},{11,9},{8,1... | collective-permute-start | bytes 135176 | tf_op jit(solution)/shard_map/ppermute | solution.py:24
  502.0 31.3 %collective-permute-start.27 = (f16[8,128,256]{2,1,0:T(8,128)(2,1)S(1)}, f16[8,128,256]{2,1,0:T(8,128)(2,1)S(1)}, u32[]{:S(2)}, u32[]{:S(2)}) collective-permute-start(f16[8,128,256]{2,1,0:T(8,128)(2,1)S(1)} %convert_element_type.109), channel_id=1, source_target_pairs={{8,0},{16,8},{24,16},{0,24},{9,1},{17,9},{25,17},{1,25},{10,2},{18... | collective-permute-start | bytes 1572872 | tf_op jit(solution)/shard_map/ppermute | solution.py:24
  505.6 10.6 %collective-permute-start.48 = (f32[8,128]{1,0:T(8,128)S(1)}, f32[8,128]{1,0:T(8,128)S(1)}, u32[]{:S(2)}, u32[]{:S(2)}) collective-permute-start(f32[8,128]{1,0:T(8,128)S(1)} %broadcast_in_dim.18), channel_id=1, source_target_pairs={{8,0},{16,8},{24,16},{0,24},{9,1},{17,9},{25,17},{1,25},{10,2},{18... | collective-permute-start | bytes 12296 | tf_op jit(solution)/shard_map/ppermute | solution.py:24
  507.3 8.9 %collective-permute-start.49 = (f32[8,128]{1,0:T(8,128)S(1)}, f32[8,128]{1,0:T(8,128)S(1)}, u32[]{:S(2)}, u32[]{:S(2)}) collective-permute-start(f32[8,128]{1,0:T(8,128)S(1)} %broadcast_in_dim.18), channel_id=1, source_target_pairs={{24,0},{0,8},{8,16},{16,24},{25,1},{1,9},{9,17},{17,25},{26,2},{2,... | collective-permute-start | bytes 12296 | tf_op jit(solution)/shard_map/ppermute | solution.py:24
  507.9 8.3 %collective-permute-start.47 = (f32[8,128]{1,0:T(8,128)S(1)}, f32[8,128]{1,0:T(8,128)S(1)}, u32[]{:S(2)}, u32[]{:S(2)}) collective-permute-start(f32[8,128]{1,0:T(8,128)S(1)} %broadcast_in_dim.18), channel_id=1, source_target_pairs={{16,0},{24,8},{0,16},{8,24},{17,1},{25,9},{1,17},{9,25},{18,2},{26... | collective-permute-start | bytes 12296 | tf_op jit(solution)/shard_map/ppermute | solution.py:24
  516.9 11.0 %collective-permute-start.51 = (f32[8,128]{1,0:T(8,128)S(1)}, f32[8,128]{1,0:T(8,128)S(1)}, u32[]{:S(2)}, u32[]{:S(2)}) collective-permute-start(f32[8,128]{1,0:T(8,128)S(1)} %add_add_fusion.7), channel_id=1, source_target_pairs={{32,0},{64,32},{96,64},{0,96},{33,1},{65,33},{97,65},{1,97},{34,2}... | collective-permute-start | bytes 12296 | tf_op jit(solution)/shard_map/ppermute | solution.py:24
  519.8 10.9 %collective-permute-start.52 = (f32[8,128]{1,0:T(8,128)S(1)}, f32[8,128]{1,0:T(8,128)S(1)}, u32[]{:S(2)}, u32[]{:S(2)}) collective-permute-start(f32[8,128]{1,0:T(8,128)S(1)} %add_add_fusion.7), channel_id=1, source_target_pairs={{96,0},{0,32},{32,64},{64,96},{97,1},{1,33},{33,65},{65,97},{98,2}... | collective-permute-start | bytes 12296 | tf_op jit(solution)/shard_map/ppermute | solution.py:24
  519.8 12.6 %collective-permute-start.50 = (f32[8,128]{1,0:T(8,128)S(1)}, f32[8,128]{1,0:T(8,128)S(1)}, u32[]{:S(2)}, u32[]{:S(2)}) collective-permute-start(f32[8,128]{1,0:T(8,128)S(1)} %add_add_fusion.7), channel_id=1, source_target_pairs={{64,0},{96,32},{0,64},{32,96},{65,1},{97,33},{1,65},{33,97},{66,2}... | collective-permute-start | bytes 12296 | tf_op jit(solution)/shard_map/ppermute | solution.py:24
  523.7 15.8 %collective-permute-start.26 = (f16[8,128,256]{2,1,0:T(8,128)(2,1)S(1)}, f16[8,128,256]{2,1,0:T(8,128)(2,1)S(1)}, u32[]{:S(2)}, u32[]{:S(2)}) collective-permute-start(f16[8,128,256]{2,1,0:T(8,128)(2,1)S(1)} %convert_element_type.107), channel_id=1, source_target_pairs={{24,0},{0,8},{8,16},{16,24},{25,1},{1,9},{9,17},{17,25},{26,2},{2,... | collective-permute-start | bytes 1572872 | tf_op jit(solution)/shard_map/ppermute | solution.py:24
  527.8 21.6 %collective-permute-start.25 = (f16[8,128,256]{2,1,0:T(8,128)(2,1)S(1)}, f16[8,128,256]{2,1,0:T(8,128)(2,1)S(1)}, u32[]{:S(2)}, u32[]{:S(2)}) collective-permute-start(f16[8,128,256]{2,1,0:T(8,128)(2,1)S(1)} %convert_element_type.105), channel_id=1, source_target_pairs={{16,0},{24,8},{0,16},{8,24},{17,1},{25,9},{1,17},{9,25},{18,2},{26... | collective-permute-start | bytes 1572872 | tf_op jit(solution)/shard_map/ppermute | solution.py:24
  530.7 18.8 %collective-permute-start.21 = (f16[8,128,256]{2,1,0:T(8,128)(2,1)S(1)}, f16[8,128,256]{2,1,0:T(8,128)(2,1)S(1)}, u32[]{:S(2)}, u32[]{:S(2)}) collective-permute-start(f16[8,128,256]{2,1,0:T(8,128)(2,1)S(1)} %convert_element_type.100), channel_id=1, source_target_pairs={{32,0},{64,32},{96,64},{0,96},{33,1},{65,33},{97,65},{1,97},{34,2}... | collective-permute-start | bytes 1572872 | tf_op jit(solution)/shard_map/ppermute | solution.py:24
  532.3 23.9 %collective-permute-start.20 = (f16[8,128,256]{2,1,0:T(8,128)(2,1)S(1)}, f16[8,128,256]{2,1,0:T(8,128)(2,1)S(1)}, u32[]{:S(2)}, u32[]{:S(2)}) collective-permute-start(f16[8,128,256]{2,1,0:T(8,128)(2,1)S(1)} %convert_element_type.98), channel_id=1, source_target_pairs={{96,0},{0,32},{32,64},{64,96},{97,1},{1,33},{33,65},{65,97},{98,2}... | collective-permute-start | bytes 1572872 | tf_op jit(solution)/shard_map/ppermute | solution.py:24
  533.3 23.0 %collective-permute-start.19 = (f16[8,128,256]{2,1,0:T(8,128)(2,1)S(1)}, f16[8,128,256]{2,1,0:T(8,128)(2,1)S(1)}, u32[]{:S(2)}, u32[]{:S(2)}) collective-permute-start(f16[8,128,256]{2,1,0:T(8,128)(2,1)S(1)} %convert_element_type.96), channel_id=1, source_target_pairs={{64,0},{96,32},{0,64},{32,96},{65,1},{97,33},{1,65},{33,97},{66,2}... | collective-permute-start | bytes 1572872 | tf_op jit(solution)/shard_map/ppermute | solution.py:24
  539.5 34.5 %collective-permute-start.53 = (f32[8,128]{1,0:T(8,128)S(1)}, f32[8,128]{1,0:T(8,128)}, u32[]{:S(2)}, u32[]{:S(2)}) collective-permute-start(f32[8,128]{1,0:T(8,128)S(1)} %add_add_fusion.6), channel_id=1, source_target_pairs={{128,0},{0,128},{129,1},{1,129},{130,2},{2,130},{131,3},{3,131},{1... | collective-permute-start | bytes 12296 | tf_op jit(solution)/shard_map/ppermute | solution.py:24
  558.6 6.7 %collective-permute-start.29 = (f16[2,128,256]{1,2,0:T(8,128)(2,1)}, f16[2,128,256]{1,2,0:T(8,128)(2,1)}, u32[]{:S(2)}, u32[]{:S(2)}) collective-permute-start(f16[2,128,256]{1,2,0:T(8,128)(2,1)} %get-tuple-element.47), channel_id=1, source_target_pairs={{96,0},{0,32},{32,64},{64,96},{97,1},{1,33},{33,65},{65,97},{98,2}... | collective-permute-start | bytes 393224 | tf_op jit(solution)/shard_map/ppermute | solution.py:24
  560.3 6.8 %collective-permute-start.28 = (f16[2,128,256]{1,2,0:T(8,128)(2,1)}, f16[2,128,256]{1,2,0:T(8,128)(2,1)}, u32[]{:S(2)}, u32[]{:S(2)}) collective-permute-start(f16[2,128,256]{1,2,0:T(8,128)(2,1)} %get-tuple-element.45), channel_id=1, source_target_pairs={{64,0},{96,32},{0,64},{32,96},{65,1},{97,33},{1,65},{33,97},{66,2}... | collective-permute-start | bytes 393224 | tf_op jit(solution)/shard_map/ppermute | solution.py:24
  562.3 5.9 %collective-permute-start.24 = (f16[2,128,256]{1,2,0:T(8,128)(2,1)S(1)}, f16[2,128,256]{1,2,0:T(8,128)(2,1)S(1)}, u32[]{:S(2)}, u32[]{:S(2)}) collective-permute-start(f16[2,128,256]{1,2,0:T(8,128)(2,1)S(1)} %get-tuple-element.43), channel_id=1, source_target_pairs={{8,0},{16,8},{24,16},{0,24},{9,1},{17,9},{25,17},{1,25},{10,2},{18... | collective-permute-start | bytes 393224 | tf_op jit(solution)/shard_map/ppermute | solution.py:24
  563.4 6.5 %collective-permute-start.23 = (f16[2,128,256]{1,2,0:T(8,128)(2,1)S(1)}, f16[2,128,256]{1,2,0:T(8,128)(2,1)S(1)}, u32[]{:S(2)}, u32[]{:S(2)}) collective-permute-start(f16[2,128,256]{1,2,0:T(8,128)(2,1)S(1)} %get-tuple-element.44), channel_id=1, source_target_pairs={{24,0},{0,8},{8,16},{16,24},{25,1},{1,9},{9,17},{17,25},{26,2},{2,... | collective-permute-start | bytes 393224 | tf_op jit(solution)/shard_map/ppermute | solution.py:24
  565.4 6.5 %collective-permute-start.22 = (f16[2,128,256]{1,2,0:T(8,128)(2,1)S(1)}, f16[2,128,256]{1,2,0:T(8,128)(2,1)S(1)}, u32[]{:S(2)}, u32[]{:S(2)}) collective-permute-start(f16[2,128,256]{1,2,0:T(8,128)(2,1)S(1)} %get-tuple-element.42), channel_id=1, source_target_pairs={{16,0},{24,8},{0,16},{8,24},{17,1},{25,9},{1,17},{9,25},{18,2},{26... | collective-permute-start | bytes 393224 | tf_op jit(solution)/shard_map/ppermute | solution.py:24
  571.9 14.3 %collective-permute-start.31 = (f32[128,512]{0,1:T(8,128)S(1)}, f32[128,512]{0,1:T(8,128)S(1)}, u32[]{:S(2)}, u32[]{:S(2)}) collective-permute-start(f32[128,512]{0,1:T(8,128)S(1)} %fusion.11), channel_id=1, source_target_pairs={{128,0},{0,128},{129,1},{1,129},{130,2},{2,130},{131,3},{3,131},{1... | collective-permute-start | bytes 786440 | tf_op jit(solution)/shard_map/ppermute | solution.py:24
  574.7 5.8 collective-permute-start.54
  (15 other events, 1055.2 us)
